TPU v7x, 32 devices: a whole 2x2x4 slice. The times are simulated.
32 devices in a mesh: dp: 8 (over z, y), tensor: 4 (over x, core).
Axes of the slice: x: 2, y: 2, z: 4, core: 2. Of those that a mesh axis runs over, the one named last changes fastest.
Arguments:
- inputs: bfloat16 [16, 1024, 768], P('dp', 'tensor'), may hold values from -6 to 6
- segment_ids: int32 [16, 1024], P('dp'), may hold values from 0 to 11, never falling along the last dimension, each value on 1 to 512 neighbouring positions
- cotangent: bfloat16 [16, 1024, 768], P('dp', 'tensor'), may hold values from -6 to 6
- w_query: bfloat16 [768, 768], P(None, 'tensor'), may hold values from -0.21875 to 0.21875
- w_key: bfloat16 [768, 768], P(None, 'tensor'), may hold values from -0.21875 to 0.21875
- w_value: bfloat16 [768, 768], P(None, 'tensor'), may hold values from -0.21875 to 0.21875
- b_query: float32 [768], P('tensor'), may hold values from -3 to 3
- b_value: float32 [768], P('tensor'), may hold values from -3 to 3
- w_out: bfloat16 [768, 768], P('tensor'), may hold values from -1.25 to 1.25
- b_out: float32 [768], replicated, may hold values from -2 to 2
- gain_one: float32 [768], replicated, may hold values from 0.5 to 1.5
- shift_one: float32 [768], replicated, may hold values from -2 to 2
- w_up: bfloat16 [768, 3072], P(None, 'tensor'), may hold values from -0.21875 to 0.21875
- b_up: float32 [3072], P('tensor'), may hold values from -3 to 3
- w_down: bfloat16 [3072, 768], P('tensor'), may hold values from -0.109375 to 0.109375
- b_down: float32 [768], replicated, may hold values from -2 to 2
- gain_two: float32 [768], replicated, may hold values from 0.5 to 1.5
- shift_two: float32 [768], replicated, may hold values from -2 to 2
Outputs:
- output: bfloat16 [16, 1024, 768], P('dp', 'tensor')
- grad_input: float32 [16, 1024, 768], P('dp', 'tensor')
- grad_w_query: float32 [768, 768], P(None, 'tensor')
- grad_w_key: float32 [768, 768], P(None, 'tensor')
- grad_w_value: float32 [768, 768], P(None, 'tensor')
- grad_b_query: float32 [768], P('tensor')
- grad_b_value: float32 [768], P('tensor')
- grad_w_out: float32 [768, 768], P('tensor')
- grad_b_out: float32 [768], replicated
- grad_gain_one: float32 [768], replicated
- grad_shift_one: float32 [768], replicated
- grad_w_up: float32 [768, 3072], P(None, 'tensor')
- grad_b_up: float32 [3072], P('tensor')
- grad_w_down: float32 [3072, 768], P('tensor')
- grad_b_down: float32 [768], replicated
- grad_gain_two: float32 [768], replicated
- grad_shift_two: float32 [768], replicated
Inputs may be any that keep to these rules, and one draw needn't show every extreme that they name: `segment_ids`: along each sequence the ids never fall; each of the 12 documents of a sequence holds 1 to 512 consecutive tokens, and some document has exactly 512 of them.
All inputs are finite; a program needn't handle non-finite values.
Results may differ from a plain program's by a relative error of at most 0.018.
Values may be sent and summed in bfloat16 or wider, within the bound.
No kernel may reach another device: no remote copies, remote signals or barrier semaphores. Data moves between devices by JAX's collectives and lax.ppermute only.
A program may use at most 128 MiB of HBM per device.

v0:
```python
import math
import jax
import jax.numpy as jnp
from jax import lax
from jax.sharding import PartitionSpec as P

HEAD_DIM = 64
LAYER_EPSILON = 1e-05
BF = jnp.bfloat16
F32 = jnp.float32


def dot(left, right, contract):
    return lax.dot_general(left, right, (contract, ((), ())), preferred_element_type=F32)


def mm(left, right):
    return dot(left, right, ((1,), (0,)))


def mm_t(left, right):
    return dot(left, right, ((1,), (1,)))


def t_mm(left, right):
    return dot(left, right, ((0,), (0,)))


def normalize(rows):
    centred = rows - jnp.mean(rows, -1, keepdims=True)
    inverse = lax.rsqrt(jnp.mean(centred * centred, -1, keepdims=True) + LAYER_EPSILON)
    return (centred * inverse, inverse)


def norm_backward(grad, gain, normal, inverse):
    scaled = grad * gain
    mean = jnp.mean(scaled, -1, keepdims=True)
    mean_z = jnp.mean(scaled * normal, -1, keepdims=True)
    return (
        inverse * (scaled - mean - normal * mean_z),
        jnp.sum(grad * normal, 0),
        jnp.sum(grad, 0),
    )


def gelu_pair(u):
    root = math.sqrt(2 / math.pi)
    t = jnp.tanh(root * (u + 0.044715 * u * u * u))
    value = 0.5 * u * (1 + t)
    slope = 0.5 * (1 + t) + 0.5 * u * (1 - t * t) * root * (1 + 3 * 0.044715 * u * u)
    return (value, slope)


def attention_forward(query, keys, values, seg_q, seg_k):
    scores = jnp.einsum("qhd,khd->hqk", query, keys, preferred_element_type=F32) / math.sqrt(
        HEAD_DIM
    )
    masked = jnp.where((seg_q[:, None] == seg_k[None, :])[None], scores, -1e30)
    top = jnp.max(masked, -1, keepdims=True)
    exponent = jnp.exp(masked - top)
    total = jnp.sum(exponent, -1, keepdims=True)
    weights = (exponent / total).astype(BF)
    context = jnp.einsum("hqk,khd->qhd", weights, values, preferred_element_type=F32)
    return (context.astype(BF), top + jnp.log(total))


def attention_backward(query, keys, values, seg_q, seg_k, logsum, grad):
    scale = 1 / math.sqrt(HEAD_DIM)
    scores = jnp.einsum("qhd,khd->hqk", query, keys, preferred_element_type=F32) * scale
    masked = jnp.where((seg_q[:, None] == seg_k[None, :])[None], scores, -1e30)
    weights = jnp.exp(masked - logsum)
    grad_weights = jnp.einsum("qhd,khd->hqk", grad, values, preferred_element_type=F32)
    row = jnp.sum(weights * grad_weights, -1, keepdims=True)
    grad_scores = (weights * (grad_weights - row)).astype(BF)
    grad_query = jnp.einsum("hqk,khd->qhd", grad_scores, keys, preferred_element_type=F32) * scale
    grad_keys = jnp.einsum("hqk,qhd->khd", grad_scores, query, preferred_element_type=F32) * scale
    grad_values = jnp.einsum("hqk,qhd->khd", weights.astype(BF), grad, preferred_element_type=F32)
    return (grad_query.astype(BF), grad_keys, grad_values)


def shards(
    inputs,
    segment_ids,
    cotangent,
    w_query,
    w_key,
    w_value,
    b_query,
    b_value,
    w_out,
    b_out,
    gain_one,
    shift_one,
    w_up,
    b_up,
    w_down,
    b_down,
    gain_two,
    shift_two,
):
    ranks = lax.axis_size("tensor")
    rank = lax.axis_index("tensor")
    which = rank % 2
    rows = inputs.shape[1]
    half = 2 * rows
    width = w_query.shape[1]
    hidden_width = w_up.shape[1]
    model = inputs.shape[2]

    def inner(x):
        return lax.ppermute(x, "tensor", [(i, i ^ 1) for i in range(ranks)])

    def outer(x):
        return lax.ppermute(x, "tensor", [(i, i ^ 2) for i in range(ranks)])

    def to_sequence(x):
        kept = jnp.where(which == 0, x[0], x[1])
        got = inner(jnp.where(which == 0, x[1], x[0]))
        return jnp.where(which == 0, jnp.concatenate([kept, got]), jnp.concatenate([got, kept]))

    def from_sequence(x):
        low, high = (x[:rows], x[rows:])
        kept = jnp.where(which == 0, low, high)
        got = inner(jnp.where(which == 0, high, low))
        return jnp.where(which == 0, jnp.stack([kept, got]), jnp.stack([got, kept]))

    own_in = to_sequence(inputs)
    other_in = outer(own_in)
    own_cot = to_sequence(cotangent).astype(F32)

    def both(x, axis):
        return jnp.concatenate([x, inner(x)], axis)

    wqkv = both(jnp.concatenate([w_query, w_key, w_value], 1)[None], 0)
    wqkv = wqkv.reshape(2, model, 3, width).transpose(1, 2, 0, 3).reshape(model, 3 * 2 * width)
    bias = both(jnp.stack([b_query, b_value])[None], 0).transpose(1, 0, 2).reshape(2, 2 * width)
    bias_qkv = jnp.concatenate([bias[0], jnp.zeros((2 * width,), F32), bias[1]])
    w_out2 = both(w_out, 0)
    w_up2 = both(w_up, 1)
    b_up2 = both(b_up, 0)
    w_down2 = both(w_down, 0)
    segments = jnp.where(which == 0, segment_ids[0], segment_ids[1])
    first = jnp.where(rank // 2 == 0, segments[:half], segments[half:])
    second = jnp.where(rank // 2 == 0, segments[half:], segments[:half])
    seg = jnp.concatenate([first, second])
    heads = 2 * width // HEAD_DIM

    def project(x):
        return (mm(x, wqkv) + bias_qkv).astype(BF)

    qkv = [project(own_in), project(other_in)]

    def split(x):
        return [
            x[:, i * 2 * width : (i + 1) * 2 * width].reshape(-1, heads, HEAD_DIM) for i in range(3)
        ]

    pieces = [split(x) for x in qkv]
    keys = jnp.concatenate([pieces[0][1], pieces[1][1]])
    values = jnp.concatenate([pieces[0][2], pieces[1][2]])
    context_other, log_other = attention_forward(pieces[1][0], keys, values, second, seg)
    context_other = context_other.reshape(half, 2 * width)
    got = outer(mm(context_other, w_out2).astype(BF))
    context_own, log_own = attention_forward(pieces[0][0], keys, values, first, seg)
    context_own = context_own.reshape(half, 2 * width)
    attended = mm(context_own, w_out2) + got.astype(F32) + b_out
    normal_one, inverse_one = normalize(own_in.astype(F32) + attended)
    hidden_one = normal_one * gain_one + shift_one
    low_own = hidden_one.astype(BF)
    low_other = outer(low_own)

    def feed(low):
        value, slope = gelu_pair(mm(low, w_up2) + b_up2)
        return (value.astype(BF), slope)

    act_own, slope_own = feed(low_own)
    act_other, slope_other = feed(low_other)
    got = outer(mm(act_other, w_down2).astype(BF))
    branch = mm(act_own, w_down2) + got.astype(F32) + b_down
    normal_two, inverse_two = normalize(hidden_one + branch)
    output = (normal_two * gain_two + shift_two).astype(BF)
    grad_two, grad_gain_two, grad_shift_two = norm_backward(
        own_cot, gain_two, normal_two, inverse_two
    )
    gb_own = grad_two.astype(BF)
    grad_b_down = jnp.sum(gb_own.astype(F32), 0)
    gb_other = outer(gb_own)
    before_own = (mm_t(gb_own, w_down2) * slope_own).astype(BF)
    before_other = (mm_t(gb_other, w_down2) * slope_other).astype(BF)
    got = outer(mm_t(before_other, w_up2).astype(BF))
    grad_w_down = t_mm(act_own, gb_own) + t_mm(act_other, gb_other)
    grad_w_up = t_mm(low_own, before_own) + t_mm(low_other, before_other)
    grad_b_up = jnp.sum(before_own.astype(F32), 0) + jnp.sum(before_other.astype(F32), 0)
    grad_hidden = mm_t(before_own, w_up2) + got.astype(F32) + grad_two
    grad_one, grad_gain_one, grad_shift_one = norm_backward(
        grad_hidden, gain_one, normal_one, inverse_one
    )
    ga_own = grad_one.astype(BF)
    grad_b_out = jnp.sum(ga_own.astype(F32), 0)
    ga_other = outer(ga_own)

    def pair_sum(mine, theirs):
        return mine + inner(theirs.astype(BF)).astype(F32)

    grad_w_up = pair_sum(grad_w_up[:, :hidden_width], grad_w_up[:, hidden_width:])
    grad_w_down = pair_sum(grad_w_down[:hidden_width], grad_w_down[hidden_width:])
    feed_flat = jnp.concatenate([grad_w_up.astype(BF), grad_w_down.astype(BF)])
    feed_flat = lax.psum(feed_flat, "dp")
    gc_own = mm_t(ga_own, w_out2).astype(BF)
    gc_other = mm_t(ga_other, w_out2).astype(BF)
    grad_w_out = t_mm(context_own, ga_own) + t_mm(context_other, ga_other)
    shaped = (half, heads, HEAD_DIM)
    gq_own, gk_a, gv_a = attention_backward(
        pieces[0][0], keys, values, first, seg, log_own, gc_own.reshape(shaped)
    )
    gq_other, gk_b, gv_b = attention_backward(
        pieces[1][0], keys, values, second, seg, log_other, gc_other.reshape(shaped)
    )
    flat = (2 * half, 2 * width)
    gk = (gk_a + gk_b).astype(BF).reshape(flat)
    gv = (gv_a + gv_b).astype(BF).reshape(flat)
    gq_own = gq_own.reshape(half, 2 * width)
    gq_other = gq_other.reshape(half, 2 * width)
    gqkv_own = jnp.concatenate([gq_own, gk[:half], gv[:half]], 1)
    gqkv_other = jnp.concatenate([gq_other, gk[half:], gv[half:]], 1)
    got = outer(mm_t(gqkv_other, wqkv).astype(BF))
    grad_wqkv = t_mm(own_in, gqkv_own) + t_mm(other_in, gqkv_other)
    grad_bqkv = jnp.sum(gqkv_own.astype(F32), 0) + jnp.sum(gqkv_other.astype(F32), 0)
    grad_input = mm_t(gqkv_own, wqkv) + got.astype(F32) + grad_one
    by_part = grad_wqkv.reshape(model, 3, 2, width)
    grad_wqkv = pair_sum(
        by_part[:, :, 0].reshape(model, 3 * width), by_part[:, :, 1].reshape(model, 3 * width)
    )
    grad_w_out = pair_sum(grad_w_out[:width], grad_w_out[width:])
    attention_flat = jnp.concatenate(
        [grad_wqkv.astype(BF).reshape(-1, model), grad_w_out.astype(BF)]
    )
    attention_flat = lax.psum(attention_flat, "dp")
    bias_parts = grad_bqkv.reshape(3, 2, width)
    mine = jnp.concatenate([bias_parts[0, 0], bias_parts[2, 0], grad_b_up[:hidden_width]])
    theirs = jnp.concatenate([bias_parts[0, 1], bias_parts[2, 1], grad_b_up[hidden_width:]])
    small = lax.psum(mine + inner(theirs), "dp")
    shared = jnp.stack(
        [grad_b_out, grad_gain_one, grad_shift_one, grad_b_down, grad_gain_two, grad_shift_two]
    )
    shared = lax.psum(shared, ("dp", "tensor"))
    gw_qkv = attention_flat[: 3 * width].reshape(model, 3, width).astype(F32)
    return (
        from_sequence(output),
        from_sequence(grad_input),
        gw_qkv[:, 0],
        gw_qkv[:, 1],
        gw_qkv[:, 2],
        small[:width],
        small[width : 2 * width],
        attention_flat[3 * width :].astype(F32),
        shared[0],
        shared[1],
        shared[2],
        feed_flat[:model].astype(F32),
        small[2 * width :],
        feed_flat[model:].astype(F32),
        shared[3],
        shared[4],
        shared[5],
    )


def solution(mesh):
    tokens = P("dp", "tensor", None)
    columns = P(None, "tensor")
    lines = P("tensor", None)
    split = P("tensor")
    whole = P()
    return jax.shard_map(
        shards,
        mesh=mesh,
        in_specs=(tokens, P("dp", None), tokens, columns, columns, columns, split, split, lines)
        + (whole, whole, whole, columns, split, lines, whole, whole, whole),
        out_specs=(
            tokens,
            tokens,
            columns,
            columns,
            columns,
            split,
            split,
            lines,
            whole,
            whole,
            whole,
        )
        + (columns, split, lines, whole, whole, whole),
        check_vma=False,
    )
```

profile of v0, /device:TPU:0, one launch (start us, length us, event | category | flops | bytes accessed | tf_op | source)
XLA Modules:
  0.0 418.1 jit_solution(3931726033955160622)
XLA Ops:
  15.8 2.6 collective-permute-start.3
  23.5 13.1 %collective-permute-done.3 = bf16[512,768]{1,0:T(8,128)(2,1)} collective-permute-done((bf16[512,768]{1,0:T(8,128)(2,1)S(1)}, bf16[512,768]{1,0:T(8,128)(2,1)}, u32[]{:S(2)}, u32[]{:S(2)}) %collective-permute-start.3) | collective-permute-done | bytes 786464 | tf_op jit(solution)/shard_map/ppermute | solution.py:114
  36.7 2.9 fusion.23
  42.2 3.6 fusion.62
  45.8 2.9 fusion.1
  48.8 2.9 fusion.45
  54.2 2.4 fusion.63
  56.6 2.6 fusion
  59.3 3.5 fusion.46
  62.7 9.0 %collective-permute-done.5 = bf16[512,768]{1,0:T(8,128)(2,1)S(1)} collective-permute-done((bf16[512,768]{1,0:T(8,128)(2,1)S(1)}, bf16[512,768]{1,0:T(8,128)(2,1)S(1)}, u32[]{:S(2)}, u32[]{:S(2)}) %collective-permute-start.5) | collective-permute-done | bytes 786464 | tf_op jit(solution)/shard_map/ppermute | solution.py:114
  81.3 10.5 %collective-permute-done.9 = bf16[512,768]{1,0:T(8,128)(2,1)S(1)} collective-permute-done((bf16[512,768]{1,0:T(8,128)(2,1)S(1)}, bf16[512,768]{1,0:T(8,128)(2,1)S(1)}, u32[]{:S(2)}, u32[]{:S(2)}) %collective-permute-start.9) | collective-permute-done | bytes 786464 | tf_op jit(solution)/shard_map/ppermute | solution.py:114
  97.8 14.9 %collective-permute-done.10 = bf16[512,768]{1,0:T(8,128)(2,1)S(1)} collective-permute-done((bf16[512,768]{1,0:T(8,128)(2,1)S(1)}, bf16[512,768]{1,0:T(8,128)(2,1)S(1)}, u32[]{:S(2)}, u32[]{:S(2)}) %collective-permute-start.10) | collective-permute-done | bytes 786464 | tf_op jit(solution)/shard_map/ppermute | solution.py:114
  116.8 2.8 convert_reduce_fusion.5
  120.5 5.9 %convert_reduce_fusion.1 = (f32[1536]{0:T(1024)}, bf16[512,1536]{1,0:T(8,128)(2,1)}) fusion(f32[512,1536]{1,0:T(8,128)} %copy-done.74, bf16[512,768]{1,0:T(8,128)(2,1)S(1)} %get-tuple-element.52, bf16[1536,768]{1,0:T(8,128)(2,1)S(1)} %constant_dynamic-update-slice_fusion.7), kind=kOutput, calls=%fused_computation.46 | convolution fusion | flops 1224473088 | bytes 7870464 | tf_op jit(solution)/shard_map/dot_general | solution.py:14
  126.4 3.0 fusion.68
  129.4 3.9 fusion.51
  133.3 3.1 collective-permute-done.13
  136.4 5.3 %convert_reduce_fusion = (f32[1536]{0:T(1024)}, bf16[512,1536]{1,0:T(8,128)(2,1)S(1)}) fusion(f32[512,1536]{1,0:T(8,128)S(1)} %convolution_add_fusion.5, bf16[512,768]{1,0:T(8,128)(2,1)} %collective-permute-done.13, bf16[1536,768]{1,0:T(8,128)(2,1)} %copy-done.53), kind=kOutput, calls=%fused_computation.45 | convolution fusion | flops 1224473088 | bytes 7870464 | tf_op jit(solution)/shard_map/dot_general | solution.py:14
  141.7 4.6 %convolution_convert_fusion = bf16[512,768]{1,0:T(8,128)(2,1)} fusion(bf16[512,1536]{1,0:T(8,128)(2,1)S(1)} %get-tuple-element.109, bf16[768,1536]{1,0:T(8,128)(2,1)} %copy-done.54), kind=kOutput, calls=%fused_computation.95 | convolution fusion | flops 1208352768 | bytes 4718592 | tf_op jit(solution)/shard_map/dot_general | solution.py:14
  146.9 5.4 %convolution_add_fusion.1 = f32[1536,768]{1,0:T(8,128)S(1)} fusion(f32[1536,768]{1,0:T(8,128)} %fusion.51, bf16[512,768]{1,0:T(8,128)(2,1)} %collective-permute-done.13, f32[512,1536]{1,0:T(8,128)} %copy-done.5), kind=kOutput, calls=%fused_computation.27 | convolution fusion | flops 1216217088 | bytes 13369344 | tf_op jit(solution)/shard_map/dot_general | solution.py:14
  155.7 3.7 convolution_add_fusion.2
  159.4 2.8 slice.342
  162.5 4.8 %multiply_reduce_fusion.2 = (f32[768]{0:T(1024)}, f32[512]{0:T(512)S(1)}, f32[512]{0:T(512)S(1)}, f32[768]{0:T(1024)}, f32[512,768]{1,0:T(8,128)S(1)}) fusion(f32[512,768]{1,0:T(8,128)S(1)} %get-tuple-element.98, f32[512]{0:T(512)S(1)} %add_rsqrt_fusion.1, f32[512]{0:T(512)S(1)} %broadcast_multiply_fusion.5, f32[768]{0:T(1024)S(1)} %copy-done.60, ...), kind=kOutput, calls=%fused_computation.78 | convolution fusion | flops 1219360256 | bytes 10252289 | tf_op jit(solution)/shard_map/dot_general | solution.py:14
  167.3 2.7 convert_reduce_fusion.6
  170.0 2.4 convolution_convert_fusion.5
  173.6 7.5 %multiply_reduce_fusion.1 = (f32[6,512]{1,0:T(8,128)}, f32[6,512,1024]{2,1,0:T(8,128)}) fusion(f32[6,512,1024]{2,1,0:T(8,128)S(1)} %get-tuple-element.96, f32[6,512]{1,0:T(8,128)S(1)} %log_add_fusion.1, bf16[512,6,64]{0,2,1:T(8,128)(2,1)} %bitcast.173, bf16[512,6,64]{0,2,1:T(8,128)(2,1)S(1)} %bitcast.149, bf16[512,6,64]{0,2,1:T(8,128)(2,1)S(1)} %bitcast.144), kind=kOutput, calls=%fused_computation.4 | convolution fusion | flops 413660160 | bytes 26370048 | tf_op jit(solution)/shard_map/qhd,khd->hqk/dot_general | solution.py:72
  181.1 9.2 %multiply_convert_fusion.1 = bf16[6,512,1024]{2,1,0:T(8,128)(2,1)} fusion(f32[6,512,1024]{2,1,0:T(8,128)} %get-tuple-element.103, f32[6,512,1024]{2,1,0:T(8,128)S(1)} %get-tuple-element.96, f32[6,512]{1,0:T(8,128)} %get-tuple-element.102, f32[6,512]{1,0:T(8,128)S(1)} %log_add_fusion.1), kind=kLoop, calls=%fused_computation.3 | loop fusion | flops 12582912 | bytes 31481856 | tf_op jit(solution)/shard_map/convert_element_type | solution.py:74
  190.4 5.7 %fusion.43 = bf16[6,64,512]{2,1,0:T(8,128)(2,1)} fusion(bf16[6,512,1024]{2,1,0:T(8,128)(2,1)} %multiply_convert_fusion.1, bf16[512,6,64]{0,2,1:T(8,128)(2,1)S(1)} %bitcast.140, bf16[512,6,64]{0,2,1:T(8,128)(2,1)S(1)} %bitcast.136), kind=kOutput, calls=%fused_computation.105 | convolution fusion | flops 404619264 | bytes 7471104 | tf_op jit(solution)/shard_map/hqk,khd->qhd/dot_general | solution.py:75
  196.1 2.8 fusion.67
  201.2 2.7 fusion.26
  206.2 3.2 fusion.4
  209.4 7.2 %multiply_reduce_fusion = (f32[6,512]{1,0:T(8,128)S(1)}, f32[6,512,1024]{2,1,0:T(8,128)}) fusion(f32[6,512,1024]{2,1,0:T(8,128)S(1)} %get-tuple-element.94, f32[6,512]{1,0:T(8,128)S(1)} %log_add_fusion, bf16[512,6,64]{0,2,1:T(8,128)(2,1)} %bitcast.176, bf16[512,6,64]{0,2,1:T(8,128)(2,1)} %bitcast.147, bf16[512,6,64]{0,2,1:T(8,128)(2,1)S(1)} %bitcast.145), kind=kOutput, calls=%fused_computation.1 | convolution fusion | flops 413660160 | bytes 26370048 | tf_op jit(solution)/shard_map/qhd,khd->hqk/dot_general | solution.py:72
  216.6 3.6 fusion.39
  220.4 6.9 %multiply_convert_fusion = bf16[6,512,1024]{2,1,0:T(8,128)(2,1)S(1)} fusion(f32[6,512,1024]{2,1,0:T(8,128)} %get-tuple-element.105, f32[6,512,1024]{2,1,0:T(8,128)S(1)} %get-tuple-element.94, f32[6,512]{1,0:T(8,128)S(1)} %get-tuple-element.104, f32[6,512]{1,0:T(8,128)S(1)} %log_add_fusion), kind=kLoop, calls=%fused_computation | loop fusion | flops 12582912 | bytes 31481856 | tf_op jit(solution)/shard_map/convert_element_type | solution.py:74
  230.7 2.5 fusion.50
  234.5 3.0 copy.63
  239.4 2.4 fusion.27
  256.5 16.2 %collective-permute-done.16 = bf16[512,768]{1,0:T(8,128)(2,1)S(1)} collective-permute-done((bf16[512,768]{1,0:T(8,128)(2,1)S(1)}, bf16[512,768]{1,0:T(8,128)(2,1)S(1)}, u32[]{:S(2)}, u32[]{:S(2)}) %collective-permute-start.16) | collective-permute-done | bytes 786464 | tf_op jit(solution)/shard_map/ppermute | solution.py:114
  275.1 42.1 %psum.30 = f32[6,768]{1,0:T(8,128)S(1)} all-reduce(f32[6,768]{1,0:T(8,128)S(1)} %stack.75), channel_id=1, replica_groups=mesh['dp'=8,'tensor'=4] {'dp','tensor'}, use_global_device_ids=true, to_apply=%region_26.27 | all-reduce | flops 4608 | bytes 36864 | tf_op jit(solution)/shard_map/psum | solution.py:246
  319.1 21.8 %psum.29 = f32[1152]{0:T(1024)S(1)} all-reduce(f32[1152]{0:T(1024)S(1)} %add.245), channel_id=1, replica_groups=mesh['dp'=8,'tensor'=4] {'dp'}, use_global_device_ids=true, to_apply=%region_19.20 | all-reduce | flops 1152 | bytes 9216 | tf_op jit(solution)/shard_map/psum | solution.py:242
  342.2 2.7 maximum_select_fusion
  344.8 45.4 %all-reduce.3.cloned.1.call-done = (bf16[768,768]{1,0:T(8,128)(2,1)}, bf16[1536,768]{1,0:T(8,128)(2,1)}) async-done(((bf16[768,768]{1,0:T(8,128)(2,1)}, bf16[1536,768]{1,0:T(8,128)(2,1)}), (bf16[768,768]{1,0:T(8,128)(2,1)}, bf16[1536,768]{1,0:T(8,128)(2,1)})) %all-reduce.3.cloned.1.call-update) | async-done | bytes 3538960 | tf_op jit(solution)/shard_map/psum | solution.py:238
  392.0 2.5 slice_convert_fusion.5
  394.5 3.5 reshape.255
  398.0 2.9 fusion.54
  401.0 3.1 copy.67
  404.0 2.9 copy.66
  408.6 2.5 slice_convert_fusion.3
  (296 shorter events, 78.8 us)
Async XLA Ops:
  7.2 383.0 %all-reduce.3.cloned.1.call-start = ((), (), s32[]{:S(2)}) async-start(), calls=%async_computation | async-start | bytes 7077888 | tf_op jit(solution)/shard_map/psum | solution.py:238
  8.0 6.6 %collective-permute-start.2 = (f32[1,2,192]{2,1,0:T(2,128)S(1)}, f32[1,2,192]{2,1,0:T(2,128)S(1)}, u32[]{:S(2)}, u32[]{:S(2)}) collective-permute-start(f32[1,2,192]{2,1,0:T(2,128)S(1)} %maximum_bitcast_fusion.1), channel_id=1, source_target_pairs={{0,1},{1,0},{2,3},{3,2},{4,5},{5,4},{6,7},{7,6},{8,9},{9,8},{10,11... | collective-permute-start | bytes 4616 | tf_op jit(solution)/shard_map/ppermute | solution.py:111
  8.6 69.0 %collective-permute-start.7 = (f32[768]{0:T(1024)}, f32[768]{0:T(1024)S(1)}, u32[]{:S(2)}, u32[]{:S(2)}) collective-permute-start(f32[768]{0:T(1024)} %param.31), channel_id=1, source_target_pairs={{0,1},{1,0},{2,3},{3,2},{4,5},{5,4},{6,7},{7,6},{8,9},{9,8},{10,11... | collective-permute-start | bytes 9224 | tf_op jit(solution)/shard_map/ppermute | solution.py:111
  8.6 7.1 %collective-permute-start.4 = (bf16[192,768]{1,0:T(8,128)(2,1)}, bf16[192,768]{1,0:T(8,128)(2,1)}, u32[]{:S(2)}, u32[]{:S(2)}) collective-permute-start(bf16[192,768]{1,0:T(8,128)(2,1)} %param.26), channel_id=1, source_target_pairs={{0,1},{1,0},{2,3},{3,2},{4,5},{5,4},{6,7},{7,6},{8,9},{9,8},{10,11... | collective-permute-start | bytes 884744 | tf_op jit(solution)/shard_map/ppermute | solution.py:111
  10.3 4.7 %collective-permute-start = (bf16[256,768]{1,0:T(8,128)(2,1)S(1)}, bf16[256,768]{1,0:T(8,128)(2,1)S(1)}, u32[]{:S(2)}, u32[]{:S(2)}) collective-permute-start(bf16[256,768]{1,0:T(8,128)(2,1)S(1)} %get-tuple-element.80), channel_id=1, source_target_pairs={{0,1},{1,0},{2,3},{3,2},{4,5},{5,4},{6,7},{7,6},{8,9},{9,8},{10,11... | collective-permute-start | bytes 1179656 | tf_op jit(solution)/shard_map/ppermute | solution.py:111
  11.5 7.9 %collective-permute-start.1 = (bf16[1,768,576]{1,2,0:T(8,128)(2,1)S(1)}, bf16[1,768,576]{1,2,0:T(8,128)(2,1)}, u32[]{:S(2)}, u32[]{:S(2)}) collective-permute-start(bf16[1,768,576]{1,2,0:T(8,128)(2,1)S(1)} %bitcast.161), channel_id=1, source_target_pairs={{0,1},{1,0},{2,3},{3,2},{4,5},{5,4},{6,7},{7,6},{8,9},{9,8},{10,11... | collective-permute-start | bytes 2654216 | tf_op jit(solution)/shard_map/ppermute | solution.py:111
  14.6 63.0 %collective-permute-start.6 = (bf16[768,768]{1,0:T(8,128)(2,1)}, bf16[768,768]{1,0:T(8,128)(2,1)}, u32[]{:S(2)}, u32[]{:S(2)}) collective-permute-start(bf16[768,768]{1,0:T(8,128)(2,1)} %param.30), channel_id=1, source_target_pairs={{0,1},{1,0},{2,3},{3,2},{4,5},{5,4},{6,7},{7,6},{8,9},{9,8},{10,11... | collective-permute-start | bytes 3538952 | tf_op jit(solution)/shard_map/ppermute | solution.py:111
  15.0 64.1 %collective-permute-start.8 = (bf16[768,768]{1,0:T(8,128)(2,1)}, bf16[768,768]{1,0:T(8,128)(2,1)}, u32[]{:S(2)}, u32[]{:S(2)}) collective-permute-start(bf16[768,768]{1,0:T(8,128)(2,1)} %param.32), channel_id=1, source_target_pairs={{0,1},{1,0},{2,3},{3,2},{4,5},{5,4},{6,7},{7,6},{8,9},{9,8},{10,11... | collective-permute-start | bytes 3538952 | tf_op jit(solution)/shard_map/ppermute | solution.py:111
  15.8 55.9 %copy-start.3 = (bf16[512,768]{1,0:T(8,128)(2,1)}, bf16[512,768]{1,0:T(8,128)(2,1)S(1)}, u32[]{:S(2)}) copy-start(bf16[512,768]{1,0:T(8,128)(2,1)S(1)} %maximum_select_fusion.1) | copy-start | bytes 2359300
  15.8 20.9 %collective-permute-start.3 = (bf16[512,768]{1,0:T(8,128)(2,1)S(1)}, bf16[512,768]{1,0:T(8,128)(2,1)}, u32[]{:S(2)}, u32[]{:S(2)}) collective-permute-start(bf16[512,768]{1,0:T(8,128)(2,1)S(1)} %maximum_select_fusion.1), channel_id=1, source_target_pairs={{0,2},{1,3},{2,0},{3,1},{4,6},{5,7},{6,4},{7,5},{8,10},{9,11},{10,... | collective-permute-start | bytes 2359304 | tf_op jit(solution)/shard_map/ppermute | solution.py:114
  23.3 167.0 %copy-start.14 = (bf16[512,384]{0,1:T(8,128)(2,1)}, bf16[512,384]{0,1:T(8,128)(2,1)S(1)}, u32[]{:S(2)}) copy-start(bf16[512,384]{0,1:T(8,128)(2,1)S(1)} %copy.60) | copy-start | bytes 1179652
  23.5 25.2 %copy-start.18 = (bf16[512,384]{0,1:T(8,128)(2,1)}, bf16[512,384]{0,1:T(8,128)(2,1)S(1)}, u32[]{:S(2)}) copy-start(bf16[512,384]{0,1:T(8,128)(2,1)S(1)} %copy.57) | copy-start | bytes 1179652
  40.7 8.1 %copy-start.22 = (bf16[512,384]{0,1:T(8,128)(2,1)}, bf16[512,384]{0,1:T(8,128)(2,1)S(1)}, u32[]{:S(2)}) copy-start(bf16[512,384]{0,1:T(8,128)(2,1)S(1)} %copy.58) | copy-start | bytes 1179652
  42.2 148.1 %copy-start.16 = (bf16[512,384]{0,1:T(8,128)(2,1)}, bf16[512,384]{0,1:T(8,128)(2,1)S(1)}, u32[]{:S(2)}) copy-start(bf16[512,384]{0,1:T(8,128)(2,1)S(1)} %copy.61) | copy-start | bytes 1179652
  52.3 19.4 %collective-permute-start.5 = (bf16[512,768]{1,0:T(8,128)(2,1)S(1)}, bf16[512,768]{1,0:T(8,128)(2,1)S(1)}, u32[]{:S(2)}, u32[]{:S(2)}) collective-permute-start(bf16[512,768]{1,0:T(8,128)(2,1)S(1)} %convolution_convert_fusion.3), channel_id=1, source_target_pairs={{0,2},{1,3},{2,0},{3,1},{4,6},{5,7},{6,4},{7,5},{8,10},{9,11},{10,... | collective-permute-start | bytes 2359304 | tf_op jit(solution)/shard_map/ppermute | solution.py:114
  59.2 12.5 %copy-start.71 = (f32[768]{0:T(1024)S(1)}, f32[768]{0:T(1024)}, u32[]{:S(2)}) copy-start(f32[768]{0:T(1024)} %param.27) | copy-start | bytes 9220
  62.7 10.1 %copy-start.40 = (bf16[6,64,512]{2,1,0:T(8,128)(2,1)}, bf16[6,64,512]{2,1,0:T(8,128)(2,1)S(1)}, u32[]{:S(2)}) copy-start(bf16[6,64,512]{2,1,0:T(8,128)(2,1)S(1)} %fusion.46) | copy-start | bytes 1179652
  73.2 18.5 %collective-permute-start.9 = (bf16[512,768]{1,0:T(8,128)(2,1)S(1)}, bf16[512,768]{1,0:T(8,128)(2,1)S(1)}, u32[]{:S(2)}, u32[]{:S(2)}) collective-permute-start(bf16[512,768]{1,0:T(8,128)(2,1)S(1)} %fusion.38), channel_id=1, source_target_pairs={{0,2},{1,3},{2,0},{3,1},{4,6},{5,7},{6,4},{7,5},{8,10},{9,11},{10,... | collective-permute-start | bytes 2359304 | tf_op jit(solution)/shard_map/ppermute | solution.py:114
  74.8 40.6 %collective-permute-start.12 = (bf16[256,768]{1,0:T(8,128)(2,1)S(1)}, bf16[256,768]{1,0:T(8,128)(2,1)S(1)}, u32[]{:S(2)}, u32[]{:S(2)}) collective-permute-start(bf16[256,768]{1,0:T(8,128)(2,1)S(1)} %get-tuple-element.75), channel_id=1, source_target_pairs={{0,1},{1,0},{2,3},{3,2},{4,5},{5,4},{6,7},{7,6},{8,9},{9,8},{10,11... | collective-permute-start | bytes 1179656 | tf_op jit(solution)/shard_map/ppermute | solution.py:111
  79.0 17.4 %copy-start.54 = (bf16[768,1536]{1,0:T(8,128)(2,1)}, bf16[768,1536]{1,0:T(8,128)(2,1)S(1)}, u32[]{:S(2)}) copy-start(bf16[768,1536]{1,0:T(8,128)(2,1)S(1)} %constant_dynamic-update-slice_fusion.5) | copy-start | bytes 7077892
  81.2 39.2 %copy-start.53 = (bf16[1536,768]{1,0:T(8,128)(2,1)}, bf16[1536,768]{1,0:T(8,128)(2,1)S(1)}, u32[]{:S(2)}) copy-start(bf16[1536,768]{1,0:T(8,128)(2,1)S(1)} %constant_dynamic-update-slice_fusion.7) | copy-start | bytes 7077892
  93.1 43.3 %copy-start.5 = (f32[512,1536]{1,0:T(8,128)}, f32[512,1536]{1,0:T(8,128)S(1)}, u32[]{:S(2)}) copy-start(f32[512,1536]{1,0:T(8,128)S(1)} %convolution_add_fusion.5) | copy-start | bytes 9437188
  95.1 17.7 %collective-permute-start.10 = (bf16[512,768]{1,0:T(8,128)(2,1)S(1)}, bf16[512,768]{1,0:T(8,128)(2,1)S(1)}, u32[]{:S(2)}, u32[]{:S(2)}) collective-permute-start(bf16[512,768]{1,0:T(8,128)(2,1)S(1)} %convolution_convert_fusion.1), channel_id=1, source_target_pairs={{0,2},{1,3},{2,0},{3,1},{4,6},{5,7},{6,4},{7,5},{8,10},{9,11},{10,... | collective-permute-start | bytes 2359304 | tf_op jit(solution)/shard_map/ppermute | solution.py:114
  96.4 16.4 %copy-start.73 = (f32[768]{0:T(1024)S(1)}, f32[768]{0:T(1024)}, u32[]{:S(2)}) copy-start(f32[768]{0:T(1024)} %param.33) | copy-start | bytes 9220
  97.8 17.3 %copy-start.74 = (f32[512,1536]{1,0:T(8,128)}, f32[512,1536]{1,0:T(8,128)S(1)}, u32[]{:S(2)}) copy-start(f32[512,1536]{1,0:T(8,128)S(1)} %convolution_add_fusion.6) | copy-start | bytes 9437188
  97.8 17.6 %copy-start.59 = (f32[768]{0:T(1024)S(1)}, f32[768]{0:T(1024)}, u32[]{:S(2)}) copy-start(f32[768]{0:T(1024)} %param.34) | copy-start | bytes 9220
  119.6 16.8 %collective-permute-start.13 = (bf16[512,768]{1,0:T(8,128)(2,1)S(1)}, bf16[512,768]{1,0:T(8,128)(2,1)}, u32[]{:S(2)}, u32[]{:S(2)}) collective-permute-start(bf16[512,768]{1,0:T(8,128)(2,1)S(1)} %get-tuple-element.52), channel_id=1, source_target_pairs={{0,2},{1,3},{2,0},{3,1},{4,6},{5,7},{6,4},{7,5},{8,10},{9,11},{10,... | collective-permute-start | bytes 2359304 | tf_op jit(solution)/shard_map/ppermute | solution.py:114
  146.3 16.2 %collective-permute-start.14 = (bf16[512,768]{1,0:T(8,128)(2,1)}, bf16[512,768]{1,0:T(8,128)(2,1)}, u32[]{:S(2)}, u32[]{:S(2)}) collective-permute-start(bf16[512,768]{1,0:T(8,128)(2,1)} %convolution_convert_fusion), channel_id=1, source_target_pairs={{0,2},{1,3},{2,0},{3,1},{4,6},{5,7},{6,4},{7,5},{8,10},{9,11},{10,... | collective-permute-start | bytes 2359304 | tf_op jit(solution)/shard_map/ppermute | solution.py:114
  153.5 9.0 %copy-start.35 = (bf16[512,1536]{1,0:T(8,128)(2,1)S(1)}, bf16[512,1536]{1,0:T(8,128)(2,1)}, u32[]{:S(2)}) copy-start(bf16[512,1536]{1,0:T(8,128)(2,1)} %get-tuple-element.107) | copy-start | bytes 4718596
  153.5 47.6 %collective-permute-start.22 = (bf16[768,768]{1,0:T(8,128)(2,1)}, bf16[768,768]{1,0:T(8,128)(2,1)}, u32[]{:S(2)}, u32[]{:S(2)}) collective-permute-start(bf16[768,768]{1,0:T(8,128)(2,1)} %slice.341), channel_id=1, source_target_pairs={{0,1},{1,0},{2,3},{3,2},{4,5},{5,4},{6,7},{7,6},{8,9},{9,8},{10,11... | collective-permute-start | bytes 3538952 | tf_op jit(solution)/shard_map/ppermute | solution.py:111
  162.3 77.1 %collective-permute-start.21 = (bf16[768,768]{1,0:T(8,128)(2,1)}, bf16[768,768]{1,0:T(8,128)(2,1)}, u32[]{:S(2)}, u32[]{:S(2)}) collective-permute-start(bf16[768,768]{1,0:T(8,128)(2,1)} %slice.342), channel_id=1, source_target_pairs={{0,1},{1,0},{2,3},{3,2},{4,5},{5,4},{6,7},{7,6},{8,9},{9,8},{10,11... | collective-permute-start | bytes 3538952 | tf_op jit(solution)/shard_map/ppermute | solution.py:111
  172.4 31.4 %collective-permute-start.15 = (bf16[512,768]{1,0:T(8,128)(2,1)}, bf16[512,768]{1,0:T(8,128)(2,1)}, u32[]{:S(2)}, u32[]{:S(2)}) collective-permute-start(bf16[512,768]{1,0:T(8,128)(2,1)} %get-tuple-element.54), channel_id=1, source_target_pairs={{0,2},{1,3},{2,0},{3,1},{4,6},{5,7},{6,4},{7,5},{8,10},{9,11},{10,... | collective-permute-start | bytes 2359304 | tf_op jit(solution)/shard_map/ppermute | solution.py:114
  190.4 8.5 %copy-start = (bf16[6,512,1024]{2,1,0:T(8,128)(2,1)S(1)}, bf16[6,512,1024]{2,1,0:T(8,128)(2,1)}, u32[]{:S(2)}) copy-start(bf16[6,512,1024]{2,1,0:T(8,128)(2,1)} %multiply_convert_fusion.1) | copy-start | bytes 18874372
  220.4 10.3 %copy-start.43 = (bf16[512,6,64]{0,2,1:T(8,128)(2,1)}, bf16[512,6,64]{0,2,1:T(8,128)(2,1)S(1)}, u32[]{:S(2)}) copy-start(bf16[512,6,64]{0,2,1:T(8,128)(2,1)S(1)} %get-tuple-element.74) | copy-start | bytes 1179652
  220.4 12.9 %copy-start.10 = (bf16[512,6,64]{0,2,1:T(8,128)(2,1)}, bf16[512,6,64]{0,2,1:T(8,128)(2,1)S(1)}, u32[]{:S(2)}) copy-start(bf16[512,6,64]{0,2,1:T(8,128)(2,1)S(1)} %get-tuple-element.73) | copy-start | bytes 1179652
  239.1 7.5 %collective-permute-start.18 = (bf16[768,576]{0,1:T(8,128)(2,1)S(1)}, bf16[768,576]{0,1:T(8,128)(2,1)S(1)}, u32[]{:S(2)}, u32[]{:S(2)}) collective-permute-start(bf16[768,576]{0,1:T(8,128)(2,1)S(1)} %bitcast.177), channel_id=1, source_target_pairs={{0,1},{1,0},{2,3},{3,2},{4,5},{5,4},{6,7},{7,6},{8,9},{9,8},{10,11... | collective-permute-start | bytes 2654216 | tf_op jit(solution)/shard_map/ppermute | solution.py:111
  243.6 3.0 collective-permute-start.19
  252.9 19.8 %copy-start.9 = (bf16[6,64,512]{2,1,0:T(8,128)(2,1)S(1)}, bf16[6,64,512]{2,1,0:T(8,128)(2,1)}, u32[]{:S(2)}) copy-start(bf16[6,64,512]{2,1,0:T(8,128)(2,1)} %fusion.43) | copy-start | bytes 1179652
  252.9 19.8 %copy-start.11 = (bf16[512,6,64]{0,2,1:T(8,128)(2,1)S(1)}, bf16[512,6,64]{0,2,1:T(8,128)(2,1)}, u32[]{:S(2)}) copy-start(bf16[512,6,64]{0,2,1:T(8,128)(2,1)} %copy-done.10) | copy-start | bytes 1179652
  253.0 19.8 %copy-start.13 = (bf16[512,6,64]{0,2,1:T(8,128)(2,1)S(1)}, bf16[512,6,64]{0,2,1:T(8,128)(2,1)}, u32[]{:S(2)}) copy-start(bf16[512,6,64]{0,2,1:T(8,128)(2,1)} %copy-done.12) | copy-start | bytes 1179652
  253.0 19.8 %copy-start.42 = (f32[512,768]{1,0:T(8,128)S(1)}, f32[512,768]{1,0:T(8,128)}, u32[]{:S(2)}) copy-start(f32[512,768]{1,0:T(8,128)} %get-tuple-element.55) | copy-start | bytes 4718596
  253.0 19.7 %collective-permute-start.16 = (bf16[512,768]{1,0:T(8,128)(2,1)S(1)}, bf16[512,768]{1,0:T(8,128)(2,1)S(1)}, u32[]{:S(2)}, u32[]{:S(2)}) collective-permute-start(bf16[512,768]{1,0:T(8,128)(2,1)S(1)} %convolution_convert_fusion.2), channel_id=1, source_target_pairs={{0,2},{1,3},{2,0},{3,1},{4,6},{5,7},{6,4},{7,5},{8,10},{9,11},{10,... | collective-permute-start | bytes 2359304 | tf_op jit(solution)/shard_map/ppermute | solution.py:114
  253.7 1.8 collective-permute-start.11
  274.0 43.2 %copy-start.45 = (bf16[512,6,64]{0,2,1:T(8,128)(2,1)S(1)}, bf16[512,6,64]{0,2,1:T(8,128)(2,1)}, u32[]{:S(2)}) copy-start(bf16[512,6,64]{0,2,1:T(8,128)(2,1)} %copy-done.43) | copy-start | bytes 1179652
  274.0 43.2 %copy-start.48 = (bf16[512,6,64]{0,2,1:T(8,128)(2,1)S(1)}, bf16[512,6,64]{0,2,1:T(8,128)(2,1)}, u32[]{:S(2)}) copy-start(bf16[512,6,64]{0,2,1:T(8,128)(2,1)} %copy-done.46) | copy-start | bytes 1179652
  275.0 67.1 %collective-permute-start.17 = (f32[256,768]{1,0:T(8,128)}, f32[256,768]{1,0:T(8,128)}, u32[]{:S(2)}, u32[]{:S(2)}) collective-permute-start(f32[256,768]{1,0:T(8,128)} %get-tuple-element.63), channel_id=1, source_target_pairs={{0,1},{1,0},{2,3},{3,2},{4,5},{5,4},{6,7},{7,6},{8,9},{9,8},{10,11... | collective-permute-start | bytes 2359304 | tf_op jit(solution)/shard_map/ppermute | solution.py:111
  317.9 1.2 collective-permute-start.20
  401.0 7.6 %copy-start.27 = (bf16[1536,768]{1,0:T(8,128)(2,1)S(1)}, bf16[1536,768]{1,0:T(8,128)(2,1)}, u32[]{:S(2)}) copy-start(bf16[1536,768]{1,0:T(8,128)(2,1)} %get-tuple-element.50) | copy-start | bytes 7077892
  (54 other events, 164.2 us)
Sparse Core Ops, SparseCore 0:
  250.1 140.0 all-reduce.2
where the time goes:
time: 425 us; the launch traced here: 418 us
  waiting for transfers between devices  114 us (27%)
  matrix products  109 us (26%)
  blocking collectives  63.9 us (15%)
  other arithmetic  54.8 us (13%)
  local copies, waits for them, and re-layouts  46.4 us (11%)
  between operations  15.6 us (4%)
  starting transfers between devices  13.8 us (3%)
    ppermute x8, waiting for transfers between devices, outer(): return lax.ppermute(x, 'tensor', [(i, i ^ 2) for i in range(ranks)])  67.1 us
    dot_general x24, matrix products, dot(): lax.dot_general(left, right, (contract, ((), ())), preferred_element_type...  63.9 us
    psum x1, waiting for transfers between devices, shards(): attention_flat = lax.psum(attention_flat, 'dp')  45.4 us
    psum x1, blocking collectives, shards(): shared = lax.psum(shared, ('dp', 'tensor'))  42.1 us
    psum x1, blocking collectives, shards(): small = lax.psum(mine + inner(theirs), 'dp')  21.8 us
    convert_element_type x2, other arithmetic, attention_backward(): grad_scores = (weights * (grad_weights - row)).astype(BF)  16.1 us
    dot_general x2, matrix products, attention_backward(): jnp.einsum('qhd,khd->hqk', grad, values, preferred_element_type=F32)  14.7 us
    unnamed x161, local copies, waits for them, and re-layouts  10.7 us
  transfers between devices with their start and end apart: 24, of which 10 were waited for; matrix products, arithmetic and copies ran while one was open for 40% of the time, Pallas kernels for 0%

commit v1 on v0

--- a/solution.py
+++ b/solution.py
@@ -8,6 +8,17 @@
 LAYER_EPSILON = 1e-05
 BF = jnp.bfloat16
 F32 = jnp.float32
+
+
+def goods_create(frame):
+    mid_arr, b_now = (frame, 0)
+    n = lax.axis_size("dp")
+    while 1 << b_now < n:
+        carry_out = tuple(((dd, dd ^ 1 << b_now) for dd in range(n)))
+        placed = lax.ppermute(mid_arr, "dp", carry_out)
+        mid_arr = mid_arr + placed
+        b_now = b_now + 1
+    return mid_arr
 
 
 def dot(left, right, contract):
@@ -235,7 +246,7 @@
     attention_flat = jnp.concatenate(
         [grad_wqkv.astype(BF).reshape(-1, model), grad_w_out.astype(BF)]
     )
-    attention_flat = lax.psum(attention_flat, "dp")
+    attention_flat = goods_create(attention_flat)
     bias_parts = grad_bqkv.reshape(3, 2, width)
     mine = jnp.concatenate([bias_parts[0, 0], bias_parts[2, 0], grad_b_up[:hidden_width]])
     theirs = jnp.concatenate([bias_parts[0, 1], bias_parts[2, 1], grad_b_up[hidden_width:]])

time: 425 us -> 469 us (1.10)
  the two profiles are of different devices: /device:TPU:0 before, /device:TPU:10 now
where the time goes in v1:
time: 469 us; the launch traced here: 462 us
  blocking collectives  137 us (29%)
  matrix products  108 us (23%)
  waiting for transfers between devices  83.4 us (18%)
  other arithmetic  59.4 us (13%)
  local copies, waits for them, and re-layouts  46.8 us (10%)
  between operations  15.6 us (3%)
  starting transfers between devices  11 us (2%)
    psum x1, blocking collectives, shards(): small = lax.psum(mine + inner(theirs), 'dp')  82.1 us
    dot_general x24, matrix products, dot(): lax.dot_general(left, right, (contract, ((), ())), preferred_element_type...  64 us
    ppermute x8, waiting for transfers between devices, outer(): return lax.ppermute(x, 'tensor', [(i, i ^ 2) for i in range(ranks)])  55.8 us
    psum x1, blocking collectives, shards(): shared = lax.psum(shared, ('dp', 'tensor'))  55.3 us
    ppermute x3, waiting for transfers between devices, goods_create(): placed = lax.ppermute(mid_arr, 'dp', carry_out)  27.5 us
    convert_element_type x2, other arithmetic, attention_backward(): grad_scores = (weights * (grad_weights - row)).astype(BF)  16.1 us
    dot_general x2, matrix products, attention_backward(): jnp.einsum('qhd,khd->hqk', grad, values, preferred_element_type=F32)  14.9 us
    unnamed x153, local copies, waits for them, and re-layouts  9.9 us
  transfers between devices with their start and end apart: 27, of which 7 were waited for; matrix products, arithmetic and copies ran while one was open for 38% of the time, Pallas kernels for 0%

profile of v1, /device:TPU:10, one launch (start us, length us, event | category | flops | bytes accessed | tf_op | source)
XLA Modules:
  0.0 462.0 jit_solution(11783263948685904958)
XLA Ops:
  21.1 14.3 %collective-permute-done.3 = bf16[512,768]{1,0:T(8,128)(2,1)} collective-permute-done((bf16[512,768]{1,0:T(8,128)(2,1)S(1)}, bf16[512,768]{1,0:T(8,128)(2,1)}, u32[]{:S(2)}, u32[]{:S(2)}) %collective-permute-start.3) | collective-permute-done | bytes 786464 | tf_op jit(solution)/shard_map/ppermute | solution.py:125
  35.4 2.9 fusion.23
  41.0 3.6 fusion.63
  44.6 2.9 fusion.1
  47.6 2.9 fusion.45
  51.7 2.4 fusion.64
  54.2 2.6 fusion
  56.8 3.5 fusion.46
  60.3 9.9 %collective-permute-done.5 = bf16[512,768]{1,0:T(8,128)(2,1)S(1)} collective-permute-done((bf16[512,768]{1,0:T(8,128)(2,1)S(1)}, bf16[512,768]{1,0:T(8,128)(2,1)S(1)}, u32[]{:S(2)}, u32[]{:S(2)}) %collective-permute-start.5) | collective-permute-done | bytes 786464 | tf_op jit(solution)/shard_map/ppermute | solution.py:125
  76.6 2.2 constant_dynamic-update-slice_fusion.7
  78.8 11.1 %collective-permute-done.9 = bf16[512,768]{1,0:T(8,128)(2,1)S(1)} collective-permute-done((bf16[512,768]{1,0:T(8,128)(2,1)S(1)}, bf16[512,768]{1,0:T(8,128)(2,1)S(1)}, u32[]{:S(2)}, u32[]{:S(2)}) %collective-permute-start.9) | collective-permute-done | bytes 786464 | tf_op jit(solution)/shard_map/ppermute | solution.py:125
  95.4 15.3 %collective-permute-done.10 = bf16[512,768]{1,0:T(8,128)(2,1)S(1)} collective-permute-done((bf16[512,768]{1,0:T(8,128)(2,1)S(1)}, bf16[512,768]{1,0:T(8,128)(2,1)S(1)}, u32[]{:S(2)}, u32[]{:S(2)}) %collective-permute-start.10) | collective-permute-done | bytes 786464 | tf_op jit(solution)/shard_map/ppermute | solution.py:125
  110.7 2.3 fusion.66
  114.7 2.8 convert_reduce_fusion.5
  118.0 5.1 %convert_reduce_fusion.1 = (f32[1536]{0:T(1024)}, bf16[512,1536]{1,0:T(8,128)(2,1)S(1)}) fusion(f32[512,1536]{1,0:T(8,128)} %copy-done.72, bf16[512,768]{1,0:T(8,128)(2,1)S(1)} %get-tuple-element.50, bf16[1536,768]{1,0:T(8,128)(2,1)S(1)} %constant_dynamic-update-slice_fusion.7), kind=kOutput, calls=%fused_computation.46 | convolution fusion | flops 1224473088 | bytes 7870464 | tf_op jit(solution)/shard_map/dot_general | solution.py:25
  125.0 3.9 fusion.52
  128.9 5.0 %collective-permute-done.13 = bf16[512,768]{1,0:T(8,128)(2,1)S(1)} collective-permute-done((bf16[512,768]{1,0:T(8,128)(2,1)S(1)}, bf16[512,768]{1,0:T(8,128)(2,1)S(1)}, u32[]{:S(2)}, u32[]{:S(2)}) %collective-permute-start.13) | collective-permute-done | bytes 786464 | tf_op jit(solution)/shard_map/ppermute | solution.py:125
  133.9 5.8 %convert_reduce_fusion = (f32[1536]{0:T(1024)}, bf16[512,1536]{1,0:T(8,128)(2,1)S(1)}) fusion(f32[512,1536]{1,0:T(8,128)} %copy-done.5, bf16[512,768]{1,0:T(8,128)(2,1)S(1)} %collective-permute-done.13, bf16[1536,768]{1,0:T(8,128)(2,1)} %copy-done.51), kind=kOutput, calls=%fused_computation.45 | convolution fusion | flops 1224473088 | bytes 7870464 | tf_op jit(solution)/shard_map/dot_general | solution.py:25
  139.8 4.5 convolution_convert_fusion
  144.8 5.4 %convolution_add_fusion.1 = f32[1536,768]{1,0:T(8,128)S(1)} fusion(f32[1536,768]{1,0:T(8,128)} %fusion.52, bf16[512,768]{1,0:T(8,128)(2,1)} %copy-done.50, f32[512,1536]{1,0:T(8,128)} %copy-done.5), kind=kOutput, calls=%fused_computation.27 | convolution fusion | flops 1216217088 | bytes 13369344 | tf_op jit(solution)/shard_map/dot_general | solution.py:25
  153.6 3.7 convolution_add_fusion.2
  157.3 2.8 slice.342
  160.2 4.8 %multiply_reduce_fusion.2 = (f32[768]{0:T(1024)}, f32[512]{0:T(512)S(1)}, f32[512]{0:T(512)S(1)}, f32[768]{0:T(1024)}, f32[512,768]{1,0:T(8,128)S(1)}) fusion(f32[512,768]{1,0:T(8,128)S(1)} %get-tuple-element.96, f32[512]{0:T(512)S(1)} %add_rsqrt_fusion.1, f32[512]{0:T(512)S(1)} %broadcast_multiply_fusion.5, f32[768]{0:T(1024)S(1)} %copy-done.58, ...), kind=kOutput, calls=%fused_computation.78 | convolution fusion | flops 1219360256 | bytes 10252289 | tf_op jit(solution)/shard_map/dot_general | solution.py:25
  165.0 2.5 convert_reduce_fusion.6
  167.6 2.4 convolution_convert_fusion.5
  171.3 7.7 %multiply_reduce_fusion.1 = (f32[6,512]{1,0:T(8,128)}, f32[6,512,1024]{2,1,0:T(8,128)}) fusion(f32[6,512,1024]{2,1,0:T(8,128)S(1)} %get-tuple-element.94, f32[6,512]{1,0:T(8,128)S(1)} %log_add_fusion.1, bf16[512,6,64]{0,2,1:T(8,128)(2,1)} %bitcast.171, bf16[512,6,64]{0,2,1:T(8,128)(2,1)S(1)} %bitcast.147, bf16[512,6,64]{0,2,1:T(8,128)(2,1)S(1)} %bitcast.142), kind=kOutput, calls=%fused_computation.4 | convolution fusion | flops 413660160 | bytes 26370048 | tf_op jit(solution)/shard_map/qhd,khd->hqk/dot_general | solution.py:83
  179.1 9.2 %multiply_convert_fusion.1 = bf16[6,512,1024]{2,1,0:T(8,128)(2,1)} fusion(f32[6,512,1024]{2,1,0:T(8,128)} %get-tuple-element.101, f32[6,512,1024]{2,1,0:T(8,128)S(1)} %get-tuple-element.94, f32[6,512]{1,0:T(8,128)} %get-tuple-element.100, f32[6,512]{1,0:T(8,128)S(1)} %log_add_fusion.1), kind=kLoop, calls=%fused_computation.3 | loop fusion | flops 12582912 | bytes 31481856 | tf_op jit(solution)/shard_map/convert_element_type | solution.py:85
  188.3 5.7 %fusion.43 = bf16[6,64,512]{2,1,0:T(8,128)(2,1)} fusion(bf16[6,512,1024]{2,1,0:T(8,128)(2,1)} %multiply_convert_fusion.1, bf16[512,6,64]{0,2,1:T(8,128)(2,1)S(1)} %bitcast.138, bf16[512,6,64]{0,2,1:T(8,128)(2,1)S(1)} %bitcast.134), kind=kOutput, calls=%fused_computation.105 | convolution fusion | flops 404619264 | bytes 7471104 | tf_op jit(solution)/shard_map/hqk,khd->qhd/dot_general | solution.py:86
  194.0 2.7 fusion.68
  200.3 3.2 fusion.4
  203.5 7.2 %multiply_reduce_fusion = (f32[6,512]{1,0:T(8,128)S(1)}, f32[6,512,1024]{2,1,0:T(8,128)}) fusion(f32[6,512,1024]{2,1,0:T(8,128)S(1)} %get-tuple-element.92, f32[6,512]{1,0:T(8,128)S(1)} %log_add_fusion, bf16[512,6,64]{0,2,1:T(8,128)(2,1)} %bitcast.174, bf16[512,6,64]{0,2,1:T(8,128)(2,1)} %bitcast.145, bf16[512,6,64]{0,2,1:T(8,128)(2,1)S(1)} %bitcast.143), kind=kOutput, calls=%fused_computation.1 | convolution fusion | flops 413660160 | bytes 26370048 | tf_op jit(solution)/shard_map/qhd,khd->hqk/dot_general | solution.py:83
  210.7 3.6 fusion.39
  214.5 6.9 %multiply_convert_fusion = bf16[6,512,1024]{2,1,0:T(8,128)(2,1)S(1)} fusion(f32[6,512,1024]{2,1,0:T(8,128)} %get-tuple-element.103, f32[6,512,1024]{2,1,0:T(8,128)S(1)} %get-tuple-element.92, f32[6,512]{1,0:T(8,128)S(1)} %get-tuple-element.102, f32[6,512]{1,0:T(8,128)S(1)} %log_add_fusion), kind=kLoop, calls=%fused_computation | loop fusion | flops 12582912 | bytes 31481856 | tf_op jit(solution)/shard_map/convert_element_type | solution.py:85
  224.8 2.6 fusion.50
  228.7 3.0 copy.63
  235.8 2.4 fusion.26
  243.8 2.2 fusion.27
  246.1 2.1 convolution_convert_fusion.2
  251.7 27.5 %collective-permute-done.20 = bf16[768,768]{1,0:T(8,128)(2,1)} collective-permute-done((bf16[768,768]{1,0:T(8,128)(2,1)}, bf16[768,768]{1,0:T(8,128)(2,1)}, u32[]{:S(2)}, u32[]{:S(2)}) %collective-permute-start.20) | collective-permute-done | bytes 1179680 | tf_op jit(solution)/shard_map/ppermute | solution.py:18
  282.7 2.4 add_add_fusion
  286.5 55.3 %psum.22 = f32[6,768]{1,0:T(8,128)} all-reduce(f32[6,768]{1,0:T(8,128)S(1)} %stack.75), channel_id=1, replica_groups=mesh['dp'=8,'tensor'=4] {'dp','tensor'}, use_global_device_ids=true, to_apply=%region_25.26 | all-reduce | flops 4608 | bytes 36864 | tf_op jit(solution)/shard_map/psum | solution.py:257
  347.6 82.1 %psum.21 = f32[1152]{0:T(1024)S(1)} all-reduce(f32[1152]{0:T(1024)S(1)} %add.255), channel_id=1, replica_groups=mesh['dp'=8,'tensor'=4] {'dp'}, use_global_device_ids=true, to_apply=%region_18.19 | all-reduce | flops 1152 | bytes 9216 | tf_op jit(solution)/shard_map/psum | solution.py:253
  431.0 3.2 maximum_select_fusion
  434.2 4.2 slice_convert_fusion.3
  440.9 3.5 reshape.255
  444.4 3.0 fusion.55
  447.4 3.0 copy.67
  450.4 2.9 copy.66
  (296 shorter events, 75.9 us)
Async XLA Ops:
  7.2 427.0 %all-reduce.2.cloned.1.call-start = ((), (), s32[]{:S(2)}) async-start(), calls=%async_computation | async-start | bytes 4718592 | tf_op jit(solution)/shard_map/psum | solution.py:219
  8.0 6.2 %collective-permute-start.2 = (f32[1,2,192]{2,1,0:T(2,128)S(1)}, f32[1,2,192]{2,1,0:T(2,128)S(1)}, u32[]{:S(2)}, u32[]{:S(2)}) collective-permute-start(f32[1,2,192]{2,1,0:T(2,128)S(1)} %maximum_bitcast_fusion.1), channel_id=1, source_target_pairs={{0,1},{1,0},{2,3},{3,2},{4,5},{5,4},{6,7},{7,6},{8,9},{9,8},{10,11... | collective-permute-start | bytes 4616 | tf_op jit(solution)/shard_map/ppermute | solution.py:122
  8.1 67.1 %collective-permute-start.7 = (f32[768]{0:T(1024)}, f32[768]{0:T(1024)S(1)}, u32[]{:S(2)}, u32[]{:S(2)}) collective-permute-start(f32[768]{0:T(1024)} %param.31), channel_id=1, source_target_pairs={{0,1},{1,0},{2,3},{3,2},{4,5},{5,4},{6,7},{7,6},{8,9},{9,8},{10,11... | collective-permute-start | bytes 9224 | tf_op jit(solution)/shard_map/ppermute | solution.py:122
  8.6 6.8 %collective-permute-start.4 = (bf16[192,768]{1,0:T(8,128)(2,1)}, bf16[192,768]{1,0:T(8,128)(2,1)}, u32[]{:S(2)}, u32[]{:S(2)}) collective-permute-start(bf16[192,768]{1,0:T(8,128)(2,1)} %param.26), channel_id=1, source_target_pairs={{0,1},{1,0},{2,3},{3,2},{4,5},{5,4},{6,7},{7,6},{8,9},{9,8},{10,11... | collective-permute-start | bytes 884744 | tf_op jit(solution)/shard_map/ppermute | solution.py:122
  9.8 5.1 %collective-permute-start = (bf16[256,768]{1,0:T(8,128)(2,1)S(1)}, bf16[256,768]{1,0:T(8,128)(2,1)S(1)}, u32[]{:S(2)}, u32[]{:S(2)}) collective-permute-start(bf16[256,768]{1,0:T(8,128)(2,1)S(1)} %get-tuple-element.78), channel_id=1, source_target_pairs={{0,1},{1,0},{2,3},{3,2},{4,5},{5,4},{6,7},{7,6},{8,9},{9,8},{10,11... | collective-permute-start | bytes 1179656 | tf_op jit(solution)/shard_map/ppermute | solution.py:122
  11.4 5.6 %collective-permute-start.1 = (bf16[1,768,576]{1,2,0:T(8,128)(2,1)S(1)}, bf16[1,768,576]{1,2,0:T(8,128)(2,1)}, u32[]{:S(2)}, u32[]{:S(2)}) collective-permute-start(bf16[1,768,576]{1,2,0:T(8,128)(2,1)S(1)} %bitcast.159), channel_id=1, source_target_pairs={{0,1},{1,0},{2,3},{3,2},{4,5},{5,4},{6,7},{7,6},{8,9},{9,8},{10,11... | collective-permute-start | bytes 2654216 | tf_op jit(solution)/shard_map/ppermute | solution.py:122
  14.2 61.0 %collective-permute-start.6 = (bf16[768,768]{1,0:T(8,128)(2,1)}, bf16[768,768]{1,0:T(8,128)(2,1)}, u32[]{:S(2)}, u32[]{:S(2)}) collective-permute-start(bf16[768,768]{1,0:T(8,128)(2,1)} %param.30), channel_id=1, source_target_pairs={{0,1},{1,0},{2,3},{3,2},{4,5},{5,4},{6,7},{7,6},{8,9},{9,8},{10,11... | collective-permute-start | bytes 3538952 | tf_op jit(solution)/shard_map/ppermute | solution.py:122
  14.9 61.7 %collective-permute-start.8 = (bf16[768,768]{1,0:T(8,128)(2,1)}, bf16[768,768]{1,0:T(8,128)(2,1)}, u32[]{:S(2)}, u32[]{:S(2)}) collective-permute-start(bf16[768,768]{1,0:T(8,128)(2,1)} %param.32), channel_id=1, source_target_pairs={{0,1},{1,0},{2,3},{3,2},{4,5},{5,4},{6,7},{7,6},{8,9},{9,8},{10,11... | collective-permute-start | bytes 3538952 | tf_op jit(solution)/shard_map/ppermute | solution.py:122
  15.4 54.8 %copy-start.3 = (bf16[512,768]{1,0:T(8,128)(2,1)}, bf16[512,768]{1,0:T(8,128)(2,1)S(1)}, u32[]{:S(2)}) copy-start(bf16[512,768]{1,0:T(8,128)(2,1)S(1)} %maximum_select_fusion.1) | copy-start | bytes 2359300
  15.4 20.0 %collective-permute-start.3 = (bf16[512,768]{1,0:T(8,128)(2,1)S(1)}, bf16[512,768]{1,0:T(8,128)(2,1)}, u32[]{:S(2)}, u32[]{:S(2)}) collective-permute-start(bf16[512,768]{1,0:T(8,128)(2,1)S(1)} %maximum_select_fusion.1), channel_id=1, source_target_pairs={{0,2},{1,3},{2,0},{3,1},{4,6},{5,7},{6,4},{7,5},{8,10},{9,11},{10,... | collective-permute-start | bytes 2359304 | tf_op jit(solution)/shard_map/ppermute | solution.py:125
  20.9 167.4 %copy-start.13 = (bf16[512,384]{0,1:T(8,128)(2,1)}, bf16[512,384]{0,1:T(8,128)(2,1)S(1)}, u32[]{:S(2)}) copy-start(bf16[512,384]{0,1:T(8,128)(2,1)S(1)} %copy.60) | copy-start | bytes 1179652
  21.1 26.4 %copy-start.17 = (bf16[512,384]{0,1:T(8,128)(2,1)}, bf16[512,384]{0,1:T(8,128)(2,1)S(1)}, u32[]{:S(2)}) copy-start(bf16[512,384]{0,1:T(8,128)(2,1)S(1)} %copy.57) | copy-start | bytes 1179652
  41.0 147.3 %copy-start.15 = (bf16[512,384]{0,1:T(8,128)(2,1)}, bf16[512,384]{0,1:T(8,128)(2,1)S(1)}, u32[]{:S(2)}) copy-start(bf16[512,384]{0,1:T(8,128)(2,1)S(1)} %copy.61) | copy-start | bytes 1179652
  51.1 19.1 %collective-permute-start.5 = (bf16[512,768]{1,0:T(8,128)(2,1)S(1)}, bf16[512,768]{1,0:T(8,128)(2,1)S(1)}, u32[]{:S(2)}, u32[]{:S(2)}) collective-permute-start(bf16[512,768]{1,0:T(8,128)(2,1)S(1)} %convolution_convert_fusion.3), channel_id=1, source_target_pairs={{0,2},{1,3},{2,0},{3,1},{4,6},{5,7},{6,4},{7,5},{8,10},{9,11},{10,... | collective-permute-start | bytes 2359304 | tf_op jit(solution)/shard_map/ppermute | solution.py:125
  56.8 13.4 %copy-start.69 = (f32[768]{0:T(1024)S(1)}, f32[768]{0:T(1024)}, u32[]{:S(2)}) copy-start(f32[768]{0:T(1024)} %param.27) | copy-start | bytes 9220
  71.7 18.2 %collective-permute-start.9 = (bf16[512,768]{1,0:T(8,128)(2,1)S(1)}, bf16[512,768]{1,0:T(8,128)(2,1)S(1)}, u32[]{:S(2)}, u32[]{:S(2)}) collective-permute-start(bf16[512,768]{1,0:T(8,128)(2,1)S(1)} %fusion.38), channel_id=1, source_target_pairs={{0,2},{1,3},{2,0},{3,1},{4,6},{5,7},{6,4},{7,5},{8,10},{9,11},{10,... | collective-permute-start | bytes 2359304 | tf_op jit(solution)/shard_map/ppermute | solution.py:125
  72.4 40.9 %collective-permute-start.12 = (bf16[256,768]{1,0:T(8,128)(2,1)S(1)}, bf16[256,768]{1,0:T(8,128)(2,1)S(1)}, u32[]{:S(2)}, u32[]{:S(2)}) collective-permute-start(bf16[256,768]{1,0:T(8,128)(2,1)S(1)} %get-tuple-element.73), channel_id=1, source_target_pairs={{0,1},{1,0},{2,3},{3,2},{4,5},{5,4},{6,7},{7,6},{8,9},{9,8},{10,11... | collective-permute-start | bytes 1179656 | tf_op jit(solution)/shard_map/ppermute | solution.py:122
  76.6 17.4 %copy-start.52 = (bf16[768,1536]{1,0:T(8,128)(2,1)}, bf16[768,1536]{1,0:T(8,128)(2,1)S(1)}, u32[]{:S(2)}) copy-start(bf16[768,1536]{1,0:T(8,128)(2,1)S(1)} %constant_dynamic-update-slice_fusion.5) | copy-start | bytes 7077892
  78.8 39.2 %copy-start.51 = (bf16[1536,768]{1,0:T(8,128)(2,1)}, bf16[1536,768]{1,0:T(8,128)(2,1)S(1)}, u32[]{:S(2)}) copy-start(bf16[1536,768]{1,0:T(8,128)(2,1)S(1)} %constant_dynamic-update-slice_fusion.7) | copy-start | bytes 7077892
  93.3 17.4 %collective-permute-start.10 = (bf16[512,768]{1,0:T(8,128)(2,1)S(1)}, bf16[512,768]{1,0:T(8,128)(2,1)S(1)}, u32[]{:S(2)}, u32[]{:S(2)}) collective-permute-start(bf16[512,768]{1,0:T(8,128)(2,1)S(1)} %convolution_convert_fusion.1), channel_id=1, source_target_pairs={{0,2},{1,3},{2,0},{3,1},{4,6},{5,7},{6,4},{7,5},{8,10},{9,11},{10,... | collective-permute-start | bytes 2359304 | tf_op jit(solution)/shard_map/ppermute | solution.py:125
  94.0 16.7 %copy-start.71 = (f32[768]{0:T(1024)S(1)}, f32[768]{0:T(1024)}, u32[]{:S(2)}) copy-start(f32[768]{0:T(1024)} %param.33) | copy-start | bytes 9220
  95.4 17.6 %copy-start.72 = (f32[512,1536]{1,0:T(8,128)}, f32[512,1536]{1,0:T(8,128)S(1)}, u32[]{:S(2)}) copy-start(f32[512,1536]{1,0:T(8,128)S(1)} %convolution_add_fusion.6) | copy-start | bytes 9437188
  95.4 18.0 %copy-start.57 = (f32[768]{0:T(1024)S(1)}, f32[768]{0:T(1024)}, u32[]{:S(2)}) copy-start(f32[768]{0:T(1024)} %param.34) | copy-start | bytes 9220
  117.5 16.4 %collective-permute-start.13 = (bf16[512,768]{1,0:T(8,128)(2,1)S(1)}, bf16[512,768]{1,0:T(8,128)(2,1)S(1)}, u32[]{:S(2)}, u32[]{:S(2)}) collective-permute-start(bf16[512,768]{1,0:T(8,128)(2,1)S(1)} %get-tuple-element.50), channel_id=1, source_target_pairs={{0,2},{1,3},{2,0},{3,1},{4,6},{5,7},{6,4},{7,5},{8,10},{9,11},{10,... | collective-permute-start | bytes 2359304 | tf_op jit(solution)/shard_map/ppermute | solution.py:125
  144.3 15.9 %collective-permute-start.14 = (bf16[512,768]{1,0:T(8,128)(2,1)}, bf16[512,768]{1,0:T(8,128)(2,1)}, u32[]{:S(2)}, u32[]{:S(2)}) collective-permute-start(bf16[512,768]{1,0:T(8,128)(2,1)} %convolution_convert_fusion), channel_id=1, source_target_pairs={{0,2},{1,3},{2,0},{3,1},{4,6},{5,7},{6,4},{7,5},{8,10},{9,11},{10,... | collective-permute-start | bytes 2359304 | tf_op jit(solution)/shard_map/ppermute | solution.py:125
  151.4 84.4 %collective-permute-start.25 = (bf16[768,768]{1,0:T(8,128)(2,1)}, bf16[768,768]{1,0:T(8,128)(2,1)}, u32[]{:S(2)}, u32[]{:S(2)}) collective-permute-start(bf16[768,768]{1,0:T(8,128)(2,1)} %slice.341), channel_id=1, source_target_pairs={{0,1},{1,0},{2,3},{3,2},{4,5},{5,4},{6,7},{7,6},{8,9},{9,8},{10,11... | collective-permute-start | bytes 3538952 | tf_op jit(solution)/shard_map/ppermute | solution.py:122
  160.1 83.7 %collective-permute-start.24 = (bf16[768,768]{1,0:T(8,128)(2,1)}, bf16[768,768]{1,0:T(8,128)(2,1)}, u32[]{:S(2)}, u32[]{:S(2)}) collective-permute-start(bf16[768,768]{1,0:T(8,128)(2,1)} %slice.342), channel_id=1, source_target_pairs={{0,1},{1,0},{2,3},{3,2},{4,5},{5,4},{6,7},{7,6},{8,9},{9,8},{10,11... | collective-permute-start | bytes 3538952 | tf_op jit(solution)/shard_map/ppermute | solution.py:122
  169.9 27.9 %collective-permute-start.15 = (bf16[512,768]{1,0:T(8,128)(2,1)}, bf16[512,768]{1,0:T(8,128)(2,1)}, u32[]{:S(2)}, u32[]{:S(2)}) collective-permute-start(bf16[512,768]{1,0:T(8,128)(2,1)} %get-tuple-element.52), channel_id=1, source_target_pairs={{0,2},{1,3},{2,0},{3,1},{4,6},{5,7},{6,4},{7,5},{8,10},{9,11},{10,... | collective-permute-start | bytes 2359304 | tf_op jit(solution)/shard_map/ppermute | solution.py:125
  214.4 13.0 %copy-start.9 = (bf16[512,6,64]{0,2,1:T(8,128)(2,1)}, bf16[512,6,64]{0,2,1:T(8,128)(2,1)S(1)}, u32[]{:S(2)}) copy-start(bf16[512,6,64]{0,2,1:T(8,128)(2,1)S(1)} %get-tuple-element.71) | copy-start | bytes 1179652
  233.4 5.4 %collective-permute-start.18 = (bf16[768,576]{0,1:T(8,128)(2,1)S(1)}, bf16[768,576]{0,1:T(8,128)(2,1)S(1)}, u32[]{:S(2)}, u32[]{:S(2)}) collective-permute-start(bf16[768,576]{0,1:T(8,128)(2,1)S(1)} %bitcast.175), channel_id=1, source_target_pairs={{0,1},{1,0},{2,3},{3,2},{4,5},{5,4},{6,7},{7,6},{8,9},{9,8},{10,11... | collective-permute-start | bytes 2654216 | tf_op jit(solution)/shard_map/ppermute | solution.py:122
  235.5 3.2 collective-permute-start.19
  242.2 36.9 %collective-permute-start.20 = (bf16[768,768]{1,0:T(8,128)(2,1)}, bf16[768,768]{1,0:T(8,128)(2,1)}, u32[]{:S(2)}, u32[]{:S(2)}) collective-permute-start(bf16[768,768]{1,0:T(8,128)(2,1)} %pad_maximum_fusion.4), channel_id=1, source_target_pairs={{0,4},{4,0},{8,12},{12,8},{16,20},{20,16},{24,28},{28,24},{1,5},{5... | collective-permute-start | bytes 3538952 | tf_op jit(solution)/shard_map/ppermute | solution.py:18
  248.2 34.5 %collective-permute-start.16 = (bf16[512,768]{1,0:T(8,128)(2,1)}, bf16[512,768]{1,0:T(8,128)(2,1)}, u32[]{:S(2)}, u32[]{:S(2)}) collective-permute-start(bf16[512,768]{1,0:T(8,128)(2,1)} %convolution_convert_fusion.2), channel_id=1, source_target_pairs={{0,2},{1,3},{2,0},{3,1},{4,6},{5,7},{6,4},{7,5},{8,10},{9,11},{10,... | collective-permute-start | bytes 2359304 | tf_op jit(solution)/shard_map/ppermute | solution.py:125
  251.4 30.2 %copy-start.56 = (f32[768]{0:T(1024)S(1)}, f32[768]{0:T(1024)}, u32[]{:S(2)}) copy-start(f32[768]{0:T(1024)} %get-tuple-element.36) | copy-start | bytes 9220
  251.4 30.2 %copy-start.60 = (f32[768]{0:T(1024)S(1)}, f32[768]{0:T(1024)}, u32[]{:S(2)}) copy-start(f32[768]{0:T(1024)} %get-tuple-element.49) | copy-start | bytes 9220
  251.4 30.2 %copy-start.59 = (f32[768]{0:T(1024)S(1)}, f32[768]{0:T(1024)}, u32[]{:S(2)}) copy-start(f32[768]{0:T(1024)} %get-tuple-element.68) | copy-start | bytes 9220
  251.5 31.2 %copy-start.62 = (f32[1536]{0:T(1024)S(1)}, f32[1536]{0:T(1024)}, u32[]{:S(2)}) copy-start(f32[1536]{0:T(1024)} %get-tuple-element.104) | copy-start | bytes 18436
  251.5 31.2 %copy-start.63 = (f32[1536]{0:T(1024)S(1)}, f32[1536]{0:T(1024)}, u32[]{:S(2)}) copy-start(f32[1536]{0:T(1024)} %get-tuple-element.106) | copy-start | bytes 18436
  251.5 31.2 %copy-start.8 = (bf16[6,64,512]{2,1,0:T(8,128)(2,1)S(1)}, bf16[6,64,512]{2,1,0:T(8,128)(2,1)}, u32[]{:S(2)}) copy-start(bf16[6,64,512]{2,1,0:T(8,128)(2,1)} %fusion.43) | copy-start | bytes 1179652
  251.5 31.2 %copy-start.10 = (bf16[512,6,64]{0,2,1:T(8,128)(2,1)S(1)}, bf16[512,6,64]{0,2,1:T(8,128)(2,1)}, u32[]{:S(2)}) copy-start(bf16[512,6,64]{0,2,1:T(8,128)(2,1)} %copy-done.9) | copy-start | bytes 1179652
  251.5 31.2 %copy-start.12 = (bf16[512,6,64]{0,2,1:T(8,128)(2,1)S(1)}, bf16[512,6,64]{0,2,1:T(8,128)(2,1)}, u32[]{:S(2)}) copy-start(bf16[512,6,64]{0,2,1:T(8,128)(2,1)} %copy-done.11) | copy-start | bytes 1179652
  251.5 31.2 %copy-start.33 = (bf16[2,768,3,192]{1,3,0,2:T(8,128)(2,1)S(1)}, bf16[2,768,3,192]{1,3,0,2:T(8,128)(2,1)}, u32[]{:S(2)}) copy-start(bf16[2,768,3,192]{1,3,0,2:T(8,128)(2,1)} %copy-done.31) | copy-start | bytes 5308420
  251.6 31.2 %copy-start.41 = (f32[512,768]{1,0:T(8,128)S(1)}, f32[512,768]{1,0:T(8,128)}, u32[]{:S(2)}) copy-start(f32[512,768]{1,0:T(8,128)} %get-tuple-element.53) | copy-start | bytes 4718596
  251.6 30.1 %collective-permute-start.11 = (bf16[256,768]{1,0:T(8,128)(2,1)S(1)}, bf16[256,768]{1,0:T(8,128)(2,1)S(1)}, u32[]{:S(2)}, u32[]{:S(2)}) collective-permute-start(bf16[256,768]{1,0:T(8,128)(2,1)S(1)} %get-tuple-element.76), channel_id=1, source_target_pairs={{0,1},{1,0},{2,3},{3,2},{4,5},{5,4},{6,7},{7,6},{8,9},{9,8},{10,11... | collective-permute-start | bytes 1179656 | tf_op jit(solution)/shard_map/ppermute | solution.py:122
  280.8 61.0 %collective-permute-start.21 = (bf16[768,768]{1,0:T(8,128)(2,1)S(1)}, bf16[768,768]{1,0:T(8,128)(2,1)}, u32[]{:S(2)}, u32[]{:S(2)}) collective-permute-start(bf16[768,768]{1,0:T(8,128)(2,1)S(1)} %fusion.51), channel_id=1, source_target_pairs={{0,8},{4,12},{8,0},{12,4},{16,24},{20,28},{24,16},{28,20},{1,9},{5... | collective-permute-start | bytes 3538952 | tf_op jit(solution)/shard_map/ppermute | solution.py:18
  286.4 144.6 %collective-permute-start.17 = (f32[256,768]{1,0:T(8,128)}, f32[256,768]{1,0:T(8,128)}, u32[]{:S(2)}, u32[]{:S(2)}) collective-permute-start(f32[256,768]{1,0:T(8,128)} %get-tuple-element.61), channel_id=1, source_target_pairs={{0,1},{1,0},{2,3},{3,2},{4,5},{5,4},{6,7},{7,6},{8,9},{9,8},{10,11... | collective-permute-start | bytes 2359304 | tf_op jit(solution)/shard_map/ppermute | solution.py:122
  343.5 94.9 %collective-permute-start.22 = (bf16[768,768]{1,0:T(8,128)(2,1)S(1)}, bf16[768,768]{1,0:T(8,128)(2,1)S(1)}, u32[]{:S(2)}, u32[]{:S(2)}) collective-permute-start(bf16[768,768]{1,0:T(8,128)(2,1)S(1)} %add.250), channel_id=1, source_target_pairs={{0,16},{4,20},{8,24},{12,28},{16,0},{20,4},{24,8},{28,12},{1,17},{... | collective-permute-start | bytes 3538952 | tf_op jit(solution)/shard_map/ppermute | solution.py:18
  345.9 1.7 collective-permute-start.23
  (53 other events, 195.0 us)
Sparse Core Ops, SparseCore 0:
  250.4 155.2 all-reduce.1
